TPU v7x, 32 devices: a whole 2x2x4 slice. The times are simulated.
32 devices in a mesh: segment: 4 (over z), mp: 4 (over y, core), tok: 2 (over x).
Axes of the slice: x: 2, y: 2, z: 4, core: 2. Of those that a mesh axis runs over, the one named last changes fastest.
Arguments:
- weights_in: bfloat16 [4, 2, 512, 32768], P('segment', None, None, 'mp'), may hold values from -0.25 to 0.25
- weights_out: bfloat16 [4, 2, 32768, 512], P('segment', None, 'mp'), may hold values from -0.03125 to 0.03125
- norm_gains: float32 [4, 2, 512], P('segment'), may hold values from 0.5 to 1.5
- activations: bfloat16 [4, 2, 2, 256, 512], P('segment', None, 'tok', 'mp'), may hold values from -6 to 6
- gradients: bfloat16 [4, 2, 2, 256, 512], P('segment', None, 'tok', 'mp'), may hold values from -6 to 6
- fresh_inputs: bfloat16 [1, 2, 256, 512], P(None, 'tok', 'mp'), may hold values from -6 to 6
- fresh_gradients: bfloat16 [1, 2, 256, 512], P(None, 'tok', 'mp'), may hold values from -6 to 6
- stashed_inputs: bfloat16 [2, 4, 2, 2, 256, 512], P(None, 'segment', None, 'tok', 'mp'), may hold values from -6 to 6
- stashed_preact: bfloat16 [2, 4, 2, 2, 256, 32768], P(None, 'segment', None, 'tok', None, 'mp'), may hold values from -6 to 6
Outputs:
- leaving_acts: bfloat16 [2, 4, 2, 2, 256, 512], P(None, 'segment', None, 'tok', 'mp')
- leaving_grads: bfloat16 [2, 4, 2, 2, 256, 512], P(None, 'segment', None, 'tok', 'mp')
All inputs are finite; a program needn't handle non-finite values.
Results may differ from a plain program's by a relative error of at most 0.014.
Values may be sent and summed in bfloat16 or wider, within the bound.
A program may use at most 128 MiB of HBM per device.

v0:
```python
import functools

import jax
import jax.numpy as jnp
from jax import lax
from jax.experimental import pallas as pl
from jax.experimental.pallas import tpu as pltpu
from jax.sharding import PartitionSpec as P

MESH = pl.DeviceIdType.MESH
EPS = 1e-06
TILE = 2048
S_TWO = 2
S_FIN = 8
ARRIVE = (22, 32, 38, 46)
ORDER = ((True, 0), (False, 0), (False, 1), (True, 1))
F0, B0, B1, F1 = range(4)


def normalize(values, gain_row):
    wide = values.astype(jnp.float32)
    inverse = lax.rsqrt(jnp.mean(wide * wide, axis=-1, keepdims=True) + EPS)
    return (wide * inverse * gain_row).astype(jnp.bfloat16)


def norm_backward(gradient, stashed, gain_row, norm_grad):
    wide = stashed.astype(jnp.float32)
    inverse = lax.rsqrt(jnp.mean(wide * wide, axis=-1, keepdims=True) + EPS)
    scaled = gain_row * norm_grad
    inner = jnp.mean(wide * scaled, axis=-1, keepdims=True)
    result = gradient.astype(jnp.float32) + inverse * scaled - wide * (inverse * inverse * inverse * inner)
    return result.astype(jnp.bfloat16)


def kernel(
    n, sections, ticks, tiles, tile,
    w_in_hbm, w_out_hbm, gains_hbm, acts_hbm, grads_hbm, fresh_a_hbm, fresh_g_hbm, stash_hbm, pre_hbm,
    out_a_hbm, out_g_hbm,
    w_in, w_out, pre, gains, rows_in, fresh, stash,
    gather, acc, own, s1_send, s1_recv, s2_send, s2_recv, outs, hop,
    w_sem, pre_sem, small_sem, far_ssem, far_rsem, near_ssem, near_rsem, s1_ssem, s1_rsem, s2_ssem, s2_rsem, hop_ssem, hop_rsem, out_sem,
):
    me = lax.axis_index("mp")
    seg = lax.axis_index("segment")
    core = lax.rem(me, 2)
    chip = me // 2
    chips = n // 2
    partner = chip * 2 + (1 - core)
    is_first = seg == 0
    is_last = seg == sections - 1
    r = rows_in.shape[2]
    passes = 4 * ticks

    def rows(block):
        return pl.ds(pl.multiple_of(block * r, r), r)

    small = [
        pltpu.make_async_copy(acts_hbm, rows_in.at[0], small_sem.at[0]),
        pltpu.make_async_copy(gains_hbm, gains, small_sem.at[1]),
        pltpu.make_async_copy(grads_hbm, rows_in.at[1], small_sem.at[2]),
        pltpu.make_async_copy(stash_hbm, stash, small_sem.at[3]),
        pltpu.make_async_copy(fresh_a_hbm, fresh.at[0], small_sem.at[4]),
        pltpu.make_async_copy(fresh_g_hbm, fresh.at[1], small_sem.at[5]),
    ]

    def w_copies(leg, i):
        cut = pl.ds(pl.multiple_of(i * tile, tile), tile)
        return (
            pltpu.make_async_copy(w_in_hbm.at[leg, :, cut], w_in.at[leg, i], w_sem.at[0, leg, i]),
            pltpu.make_async_copy(w_out_hbm.at[leg, cut, :], w_out.at[leg, i], w_sem.at[1, leg, i]),
        )

    def pre_copy(t, leg, i):
        cut = pl.ds(pl.multiple_of(i * tile, tile), tile)
        return pltpu.make_async_copy(pre_hbm.at[t, leg, :, cut], pre.at[2 * t + leg, i], pre_sem.at[2 * t + leg, i])

    small[0].start()
    small[1].start()
    small[2].start()
    for copy in w_copies(0, 0):
        copy.start()
    for copy in small[3:]:
        copy.start()

    barrier = pltpu.get_barrier_semaphore()
    for d in range(1, n):
        pl.semaphore_signal(barrier, inc=1, device_id={"mp": lax.rem(me + d, n)}, device_id_type=MESH)

    @pl.when(seg > 0)
    def _():
        pl.semaphore_signal(barrier, inc=1, device_id={"segment": seg - 1}, device_id_type=MESH)

    @pl.when(seg < sections - 1)
    def _():
        pl.semaphore_signal(barrier, inc=1, device_id={"segment": seg + 1}, device_id_type=MESH)

    peers = n - 1 + (seg > 0).astype(jnp.int32) + (seg < sections - 1).astype(jnp.int32)
    pl.semaphore_wait(barrier, peers)

    def far_copy(p, d):
        return pltpu.make_async_remote_copy(
            src_ref=gather.at[p, rows(me)], dst_ref=gather.at[p, rows(me)],
            send_sem=far_ssem.at[p, d - 1], recv_sem=far_rsem.at[p, d - 1],
            device_id={"mp": lax.rem(chip + d, chips) * 2 + core}, device_id_type=MESH,
        )

    def near_copy(p, d):
        block = lax.rem(chip + chips - d, chips) * 2 + core
        return pltpu.make_async_remote_copy(
            src_ref=gather.at[p, rows(block)], dst_ref=gather.at[p, rows(block)],
            send_sem=near_ssem.at[p, d], recv_sem=near_rsem.at[p, d],
            device_id={"mp": partner}, device_id_type=MESH,
        )

    def s1_copy(p):
        return pltpu.make_async_remote_copy(
            src_ref=s1_send.at[p], dst_ref=s1_recv.at[p],
            send_sem=s1_ssem.at[p], recv_sem=s1_rsem.at[p],
            device_id={"mp": partner}, device_id_type=MESH,
        )

    def s2_copy(p, d):
        return pltpu.make_async_remote_copy(
            src_ref=s2_send.at[p, d - 1], dst_ref=s2_recv.at[p, d - 1],
            send_sem=s2_ssem.at[p, d - 1], recv_sem=s2_rsem.at[p, d - 1],
            device_id={"mp": lax.rem(chip + d, chips) * 2 + core}, device_id_type=MESH,
        )

    def hop_copy(p):
        step = 1 if p % 4 in (F0, B1) else -1
        return pltpu.make_async_remote_copy(
            src_ref=outs.at[p], dst_ref=hop.at[p],
            send_sem=hop_ssem.at[p], recv_sem=hop_rsem.at[p],
            device_id={"segment": seg + step}, device_id_type=MESH,
        )

    def hop_sends(p):
        return jnp.logical_not(is_last) if p % 4 in (F0, B1) else jnp.logical_not(is_first)

    def hop_arrives(p):
        return jnp.logical_not(is_first) if p % 4 in (F0, B1) else jnp.logical_not(is_last)

    def out_copy(p):
        t, (forward, leg) = p // 4, ORDER[p % 4]
        return pltpu.make_async_copy(
            outs.at[p], (out_a_hbm if forward else out_g_hbm).at[t, leg], out_sem.at[p]
        )

    def rows_ref(p):
        forward, leg = ORDER[p % 4]
        return rows_in.at[2 * (p // 4) + (0 if forward else 1), leg]

    def enter(p):
        forward, leg = ORDER[p % 4]
        values = rows_ref(p)[...]
        gather[p, rows(me)] = normalize(values, gains[pl.ds(leg, 1), :]) if forward else values
        for d in range(1, chips):
            far_copy(p, d).start()
        near_copy(p, 0).start()

    def relay(p):
        for d in range(1, chips):
            far_copy(p, d).wait_recv()
            near_copy(p, d).start()

    def arrive(p):
        t, kind = p // 4, p % 4
        before = p - 4
        target = rows_ref(p)

        @pl.when(hop_arrives(before))
        def _():
            hop_copy(before).wait_recv()
            target[...] = hop[before]

        @pl.when(jnp.logical_not(hop_arrives(before)))
        def _():
            if kind == F0:
                target[...] = fresh[0, t - 1]
            elif kind == B1:
                target[...] = fresh[1, t - 1]
            elif kind == F1:
                target[...] = outs[before - F1 + F0]
            else:
                target[...] = outs[before - B0 + B1]

        enter(p)

    def scatter_one(p):
        for c in range(chips):
            s1_send[p, c] = acc[p % 2, rows(2 * c + (1 - core))].astype(jnp.bfloat16)
        s1_copy(p).start()

    def scatter_two(p):
        s1_copy(p).wait_recv()
        for d in range(1, chips):
            other = lax.rem(chip + d, chips)
            s2_send[p, d - 1] = (
                acc[p % 2, rows(2 * other + core)] + s1_recv[p, other].astype(jnp.float32)
            ).astype(jnp.bfloat16)
            s2_copy(p, d).start()
        own[p] = acc[p % 2, rows(me)] + s1_recv[p, chip].astype(jnp.float32)

    def finish(p):
        t, (forward, leg) = p // 4, ORDER[p % 4]
        total = own[p]
        for d in range(1, chips):
            s2_copy(p, d).wait_recv()
            total = total + s2_recv[p, d - 1].astype(jnp.float32)
        entered = rows_ref(p)[...]
        if forward:
            outs[p] = (entered.astype(jnp.float32) + total).astype(jnp.bfloat16)
        else:
            outs[p] = norm_backward(entered, stash[t, leg], gains[pl.ds(leg, 1), :], total)
        out_copy(p).start()
        if t + 1 < ticks:
            @pl.when(hop_sends(p))
            def _():
                hop_copy(p).start()

    hooks = [[] for _ in range(passes + 1)]
    order = []

    def at(p, eighth, call):
        key = (8 * p + eighth, len(order))
        order.append(key)
        hooks[min(p, passes)].append((min(eighth * tiles // 8, tiles - 1), key, call))

    at(0, 4, lambda: (small[3].wait(), small[4].wait(), small[5].wait(), enter(B1)))
    at(0, 6, lambda: relay(B0))
    at(1, 0, lambda: enter(F1))
    at(1, 2, lambda: relay(B1))
    at(1, 6, lambda: relay(F1))
    for p in range(passes):
        at(p + 1, S_TWO, functools.partial(scatter_two, p))
        at(p + 1 + S_FIN // 8, S_FIN % 8, functools.partial(finish, p))
    for t in range(1, ticks):
        for kind in range(4):
            slot = ARRIVE[kind]
            at(4 * t - 4 + slot // 8, slot % 8, functools.partial(arrive, 4 * t + kind))
            at(4 * t - 4 + (slot + 6) // 8, (slot + 6) % 8, functools.partial(relay, 4 * t + kind))
    for entry in hooks:
        entry.sort(key=lambda item: item[1])

    small[0].wait()
    small[1].wait()
    enter(F0)
    for i in range(1, tiles):
        for copy in w_copies(0, i):
            copy.start()
    for i in range(tiles):
        pre_copy(0, 0, i).start()
    for i in range(tiles):
        pre_copy(0, 1, i).start()
        for copy in w_copies(1, i):
            copy.start()
    relay(F0)
    small[2].wait()
    enter(B0)

    for p in range(passes):
        t, (forward, leg) = p // 4, ORDER[p % 4]
        first_use = t == 0 and p % 4 in (F0, B1)
        for d in range(chips):
            near_copy(p, d).wait_recv()
        acc[p % 2] = jnp.zeros_like(acc[p % 2])

        def step(i, carry, p=p, t=t, forward=forward, leg=leg, first_use=first_use):
            if p % 4 == B0 and t + 1 < ticks:
                pre_copy(t + 1, 0, i).start()
                pre_copy(t + 1, 1, i).start()
            for where, _, call in hooks[p]:
                pl.when(i == where)(lambda call=call: (call(), None)[1])
            if first_use:
                for copy in w_copies(leg, i):
                    copy.wait()
            x = gather[p]
            if forward:
                hidden = jnp.maximum(jnp.dot(x, w_in[leg, i], preferred_element_type=jnp.float32), 0.0)
                acc[p % 2] += jnp.dot(hidden.astype(jnp.bfloat16), w_out[leg, i], preferred_element_type=jnp.float32)
            else:
                pre_copy(t, leg, i).wait()
                up = lax.dot_general(
                    x, w_out[leg, i], (((1,), (1,)), ((), ())), preferred_element_type=jnp.float32
                )
                masked = jnp.where(pre[2 * t + leg, i].astype(jnp.float32) > 0, up, 0.0).astype(jnp.bfloat16)
                acc[p % 2] += lax.dot_general(
                    masked, w_in[leg, i], (((1,), (1,)), ((), ())), preferred_element_type=jnp.float32
                )
            return carry

        lax.fori_loop(0, tiles, step, 0)
        scatter_one(p)

    for _, _, call in hooks[passes]:
        call()

    for p in range(passes):
        for d in range(1, chips):
            far_copy(p, d).wait_send()
        for d in range(chips):
            near_copy(p, d).wait_send()
        s1_copy(p).wait_send()
        for d in range(1, chips):
            s2_copy(p, d).wait_send()
        if p // 4 + 1 < ticks:
            @pl.when(hop_sends(p))
            def _():
                hop_copy(p).wait_send()
        out_copy(p).wait()


def flush(a_ref, g_ref, out_a_ref, out_g_ref, held, sem):
    pairs = ((a_ref, out_a_ref), (g_ref, out_g_ref))
    loads = [pltpu.make_async_copy(src, held.at[k], sem.at[0, k]) for k, (src, _) in enumerate(pairs)]
    stores = [pltpu.make_async_copy(held.at[k], dst, sem.at[1, k]) for k, (_, dst) in enumerate(pairs)]
    for copy in loads:
        copy.start()
    for load, store in zip(loads, stores):
        load.wait()
        store.start()
    for copy in stores:
        copy.wait()


def body(n, sections, w_in, w_out, gains, acts, grads, fresh_a, fresh_g, stash, pre):
    ticks = stash.shape[0]
    _, legs, d, ff = w_in.shape
    r = acts.shape[3]
    total_rows = n * r
    tile = min(TILE, ff)
    tiles = ff // tile
    chips = n // 2
    passes = 4 * ticks
    bf16, f32 = jnp.bfloat16, jnp.float32
    any_spec = pl.BlockSpec(memory_space=pl.ANY)
    dma = pltpu.SemaphoreType.DMA
    far = max(chips - 1, 1)
    out = jax.ShapeDtypeStruct((ticks, legs, r, d), bf16)
    out_a, out_g = pl.pallas_call(
        functools.partial(kernel, n, sections, ticks, tiles, tile),
        out_shape=(out, out),
        in_specs=[any_spec] * 9,
        out_specs=(any_spec, any_spec),
        scratch_shapes=[
            pltpu.VMEM((legs, tiles, d, tile), bf16),
            pltpu.VMEM((legs, tiles, tile, d), bf16),
            pltpu.VMEM((ticks * legs, tiles, total_rows, tile), bf16),
            pltpu.VMEM((legs, d), f32),
            pltpu.VMEM((2 * ticks, legs, r, d), bf16),
            pltpu.VMEM((2,) + (max(ticks - 1, 1), r, d), bf16),
            pltpu.VMEM((ticks, legs, r, d), bf16),
            pltpu.VMEM((passes, total_rows, d), bf16),
            pltpu.VMEM((2, total_rows, d), f32),
            pltpu.VMEM((passes, r, d), f32),
            pltpu.VMEM((passes, chips, r, d), bf16),
            pltpu.VMEM((passes, chips, r, d), bf16),
            pltpu.VMEM((passes, far, r, d), bf16),
            pltpu.VMEM((passes, far, r, d), bf16),
            pltpu.VMEM((passes, r, d), bf16),
            pltpu.VMEM((passes, r, d), bf16),
            dma((2, legs, tiles)),
            dma((ticks * legs, tiles)),
            dma((6,)),
            dma((passes, far)),
            dma((passes, far)),
            dma((passes, chips)),
            dma((passes, chips)),
            dma((passes,)),
            dma((passes,)),
            dma((passes, far)),
            dma((passes, far)),
            dma((passes,)),
            dma((passes,)),
            dma((passes,)),
        ],
        compiler_params=pltpu.CompilerParams(
            collective_id=0, has_side_effects=True, vmem_limit_bytes=67043328
        ),
        name="relay",
    )(
        w_in[0], w_out[0], gains[0], acts[0, :, 0], grads[0, :, 0],
        fresh_a[:, 0], fresh_g[:, 0], stash[:, 0, :, 0], pre[:, 0, :, 0],
    )
    out_a, out_g = pl.pallas_call(
        flush,
        out_shape=(out, out),
        in_specs=[any_spec] * 2,
        out_specs=(any_spec, any_spec),
        scratch_shapes=[pltpu.VMEM((2,) + out.shape, bf16), dma((2, 2))],
        name="flush",
    )(out_a, out_g)
    return out_a[:, None, :, None], out_g[:, None, :, None]


def solution(mesh):
    return jax.shard_map(
        functools.partial(body, mesh.shape["mp"], mesh.shape["segment"]),
        mesh=mesh,
        in_specs=(
            P("segment", None, None, "mp"),
            P("segment", None, "mp", None),
            P("segment", None, None),
            P("segment", None, "tok", "mp", None),
            P("segment", None, "tok", "mp", None),
            P(None, "tok", "mp", None),
            P(None, "tok", "mp", None),
            P(None, "segment", None, "tok", "mp", None),
            P(None, "segment", None, "tok", None, "mp"),
        ),
        out_specs=(
            P(None, "segment", None, "tok", "mp", None),
            P(None, "segment", None, "tok", "mp", None),
        ),
        check_vma=False,
    )
```

profile of v0, /device:TPU:0, one launch (start us, length us, event | category | flops | bytes accessed | tf_op | source)
XLA Modules:
  0.0 59.6 jit_solution(17608896605056367800)
XLA Ops:
  0.6 57.2 %relay.1 = (bf16[2,2,64,512]{3,2,1,0:T(8,128)(2,1)}, bf16[2,2,64,512]{3,2,1,0:T(8,128)(2,1)}) custom-call(bf16[2,512,8192]{2,1,0:T(8,128)(2,1)} %bitcast.15, bf16[2,8192,512]{2,1,0:T(8,128)(2,1)} %bitcast.16, f32[2,512]{1,0:T(2,128)} %bitcast.23, bf16[2,64,512]{2,1,0:T(8,128)(2,1)} %bitcast.19, bf16[2,64,512]{2,1,0:T(8,128)(2,1)} %bitcast.20, ...), custom_call_target="tpu_custom_call" | custom-call | tf_op jit(solution)/shard_map/relay/pallas_call | solution.py:340
  57.8 1.8 %flush.1 = (bf16[2,2,64,512]{3,2,1,0:T(8,128)(2,1)}, bf16[2,2,64,512]{3,2,1,0:T(8,128)(2,1)}) custom-call(bf16[2,2,64,512]{3,2,1,0:T(8,128)(2,1)} %get-tuple-element.6.a_ref, bf16[2,2,64,512]{3,2,1,0:T(8,128)(2,1)} %get-tuple-element.7.g_ref), custom_call_target="tpu_custom_call" | custom-call | tf_op jit(solution)/shard_map/flush/pallas_call | solution.py:385
where the time goes:
time: 59.8 us; the launch traced here: 59.6 us
  Pallas kernels  59 us (99%)
  between operations  0.64 us (1%)
    pallas_call x1, Pallas kernels, body(): pl.pallas_call(functools.partial(kernel, n, sections, ticks, tiles, tile)...  57.2 us
    pallas_call x1, Pallas kernels, body(): pl.pallas_call(flush, out_shape=(out, out), in_specs=[any_spec] * 2, out_...  1.77 us

commit v1 on v0

v1 whole, which is shorter than its diff:
```python
import functools

import jax
import jax.numpy as jnp
from jax import lax
from jax.experimental import pallas as pl
from jax.experimental.pallas import tpu as pltpu
from jax.sharding import PartitionSpec as P

MESH = pl.DeviceIdType.MESH
EPS = 1e-06
QUARTERS = 4
ORDER = ((True, 0), (False, 0), (False, 1), (True, 1))
F0, B0, B1, F1 = range(4)


def normalize(values, gain_row):
    wide = values.astype(jnp.float32)
    inverse = lax.rsqrt(jnp.mean(wide * wide, axis=-1, keepdims=True) + EPS)
    return (wide * inverse * gain_row).astype(jnp.bfloat16)


def norm_backward(gradient, stashed, gain_row, norm_grad):
    wide = stashed.astype(jnp.float32)
    inverse = lax.rsqrt(jnp.mean(wide * wide, axis=-1, keepdims=True) + EPS)
    scaled = gain_row * norm_grad
    inner = jnp.mean(wide * scaled, axis=-1, keepdims=True)
    result = gradient.astype(jnp.float32) + inverse * scaled - wide * (inverse * inverse * inverse * inner)
    return result.astype(jnp.bfloat16)


def kernel(
    n, sections, ticks,
    w_in_hbm, w_out_hbm, gains_hbm, acts_hbm, grads_hbm, fresh_a_hbm, fresh_g_hbm, stash_hbm, pre_hbm,
    out_a_hbm, out_g_hbm,
    w_in, w_out, pre, gains, rows_in, fresh, stash,
    gather, acc, own, s1_send, s1_recv, s2_send, s2_recv, outs, hop,
    w_sem, pre_sem, small_sem, far_ssem, far_rsem, near_ssem, near_rsem, s1_ssem, s1_rsem, s2_ssem, s2_rsem, hop_ssem, hop_rsem, out_sem,
):
    me = lax.axis_index("mp")
    seg = lax.axis_index("segment")
    core = lax.rem(me, 2)
    chip = me // 2
    chips = n // 2
    partner = chip * 2 + (1 - core)
    is_first = seg == 0
    is_last = seg == sections - 1
    r = rows_in.shape[2]
    quarter = w_in.shape[2] // QUARTERS
    near_rows = slice(0, 2 * r)
    far_rows = slice(2 * r, n * r)

    def rows(k, which):
        return pl.ds(pl.multiple_of((2 * k + which) * r, r), r)

    small = [
        pltpu.make_async_copy(acts_hbm, rows_in.at[0], small_sem.at[0]),
        pltpu.make_async_copy(gains_hbm, gains, small_sem.at[1]),
        pltpu.make_async_copy(grads_hbm, rows_in.at[1], small_sem.at[2]),
        pltpu.make_async_copy(stash_hbm, stash, small_sem.at[3]),
        pltpu.make_async_copy(fresh_a_hbm, fresh.at[0], small_sem.at[4]),
        pltpu.make_async_copy(fresh_g_hbm, fresh.at[1], small_sem.at[5]),
    ]

    def w_copies(leg, i):
        cut = pl.ds(i * quarter, quarter)
        return (
            pltpu.make_async_copy(w_in_hbm.at[leg, :, cut], w_in.at[leg, :, cut], w_sem.at[0, leg, i]),
            pltpu.make_async_copy(w_out_hbm.at[leg, cut, :], w_out.at[leg, cut, :], w_sem.at[1, leg, i]),
        )

    def pre_copies(t, leg, i):
        cut = pl.ds(i * quarter, quarter)
        return [
            pltpu.make_async_copy(
                pre_hbm.at[t, leg, pl.ds(pl.multiple_of(lax.rem(chip + k, chips) * 2 * r, 2 * r), 2 * r), cut],
                pre.at[2 * t + leg, pl.ds(2 * k * r, 2 * r), cut],
                pre_sem.at[2 * t + leg, i, k],
            )
            for k in range(chips)
        ]

    small[0].start()
    small[1].start()
    small[2].start()
    for i in range(QUARTERS):
        for copy in w_copies(0, i):
            copy.start()
    for copy in small[3:]:
        copy.start()

    barrier = pltpu.get_barrier_semaphore()
    for d in range(1, n):
        pl.semaphore_signal(barrier, inc=1, device_id={"mp": lax.rem(me + d, n)}, device_id_type=MESH)

    @pl.when(seg > 0)
    def _():
        pl.semaphore_signal(barrier, inc=1, device_id={"segment": seg - 1}, device_id_type=MESH)

    @pl.when(seg < sections - 1)
    def _():
        pl.semaphore_signal(barrier, inc=1, device_id={"segment": seg + 1}, device_id_type=MESH)

    peers = n - 1 + (seg > 0).astype(jnp.int32) + (seg < sections - 1).astype(jnp.int32)
    pl.semaphore_wait(barrier, peers)

    def far_copy(p, d):
        return pltpu.make_async_remote_copy(
            src_ref=gather.at[p, rows(0, core)], dst_ref=gather.at[p, rows(chips - d, core)],
            send_sem=far_ssem.at[p, d - 1], recv_sem=far_rsem.at[p, d - 1],
            device_id={"mp": lax.rem(chip + d, chips) * 2 + core}, device_id_type=MESH,
        )

    def near_copy(p, k):
        return pltpu.make_async_remote_copy(
            src_ref=gather.at[p, rows(k, core)], dst_ref=gather.at[p, rows(k, core)],
            send_sem=near_ssem.at[p, k], recv_sem=near_rsem.at[p, k],
            device_id={"mp": partner}, device_id_type=MESH,
        )

    def s1_copy(p, part):
        cut = pl.ds(0, 1) if part == 0 else pl.ds(1, chips - 1)
        return pltpu.make_async_remote_copy(
            src_ref=s1_send.at[p, cut], dst_ref=s1_recv.at[p, cut],
            send_sem=s1_ssem.at[p, part], recv_sem=s1_rsem.at[p, part],
            device_id={"mp": partner}, device_id_type=MESH,
        )

    def s2_copy(p, d):
        return pltpu.make_async_remote_copy(
            src_ref=s2_send.at[p, d - 1], dst_ref=s2_recv.at[p, d - 1],
            send_sem=s2_ssem.at[p, d - 1], recv_sem=s2_rsem.at[p, d - 1],
            device_id={"mp": lax.rem(chip + d, chips) * 2 + core}, device_id_type=MESH,
        )

    def hop_copy(t, kind):
        p = 4 * t + kind
        step = 1 if kind in (F0, B1) else -1
        return pltpu.make_async_remote_copy(
            src_ref=outs.at[p], dst_ref=hop.at[p],
            send_sem=hop_ssem.at[p], recv_sem=hop_rsem.at[p],
            device_id={"segment": seg + step}, device_id_type=MESH,
        )

    def hop_sends(kind):
        return jnp.logical_not(is_last) if kind in (F0, B1) else jnp.logical_not(is_first)

    def hop_arrives(kind):
        return jnp.logical_not(is_first) if kind in (F0, B1) else jnp.logical_not(is_last)

    def out_copy(t, kind):
        forward, leg = ORDER[kind]
        p = 4 * t + kind
        return pltpu.make_async_copy(
            outs.at[p], (out_a_hbm if forward else out_g_hbm).at[t, leg], out_sem.at[p]
        )

    def rows_ref(t, kind):
        forward, leg = ORDER[kind]
        return rows_in.at[2 * t + (0 if forward else 1), leg]

    def enter(t, kind):
        forward, leg = ORDER[kind]
        p = 4 * t + kind
        values = rows_ref(t, kind)[...]
        gather[p, rows(0, core)] = normalize(values, gains[pl.ds(leg, 1), :]) if forward else values
        for d in range(1, chips):
            far_copy(p, d).start()
        near_copy(p, 0).start()

    def relay(t, kind):
        p = 4 * t + kind
        for d in range(1, chips):
            far_copy(p, d).wait_recv()
            near_copy(p, chips - d).start()

    def arrive(t, kind):
        target = rows_ref(t, kind)
        before = 4 * t - 4

        @pl.when(hop_arrives(kind))
        def _():
            hop_copy(t - 1, kind).wait_recv()
            target[...] = hop[before + kind]

        @pl.when(jnp.logical_not(hop_arrives(kind)))
        def _():
            if kind == F0:
                target[...] = fresh[0, t - 1]
            elif kind == B1:
                target[...] = fresh[1, t - 1]
            elif kind == F1:
                target[...] = outs[before + F0]
            else:
                target[...] = outs[before + B1]

        enter(t, kind)

    def scatter_one(t, kind, part):
        p = 4 * t + kind
        for k in range(1) if part == 0 else range(1, chips):
            s1_send[p, k] = acc[kind % 2, rows(k, 1 - core)].astype(jnp.bfloat16)
        s1_copy(p, part).start()

    def scatter_far(t, kind):
        p = 4 * t + kind
        s1_copy(p, 1).wait_recv()
        for d in range(1, chips):
            s2_send[p, d - 1] = (
                acc[kind % 2, rows(d, core)] + s1_recv[p, d].astype(jnp.float32)
            ).astype(jnp.bfloat16)
            s2_copy(p, d).start()

    def scatter_own(t, kind):
        p = 4 * t + kind
        s1_copy(p, 0).wait_recv()
        own[p] = acc[kind % 2, rows(0, core)] + s1_recv[p, 0].astype(jnp.float32)

    def scatter_two(t, kind):
        scatter_far(t, kind)
        scatter_own(t, kind)

    def finish(t, kind):
        forward, leg = ORDER[kind]
        p = 4 * t + kind
        total = own[p]
        for d in range(1, chips):
            s2_copy(p, d).wait_recv()
            total = total + s2_recv[p, d - 1].astype(jnp.float32)
        entered = rows_ref(t, kind)[...]
        if forward:
            outs[p] = (entered.astype(jnp.float32) + total).astype(jnp.bfloat16)
        else:
            outs[p] = norm_backward(entered, stash[t, leg], gains[pl.ds(leg, 1), :], total)
        out_copy(t, kind).start()

        @pl.when(jnp.logical_and(t + 1 < ticks, hop_sends(kind)))
        def _():
            hop_copy(t, kind).start()

    def first(t, call):
        pl.when(t == 0)(lambda: (call(), None)[1])

    def later(t, call):
        pl.when(t > 0)(lambda: (call(), None)[1])

    def more(t, call):
        pl.when(t + 1 < ticks)(lambda: (call(), None)[1])

    def near_ready(t, kind):
        near_copy(4 * t + kind, 0).wait_recv()

    def far_ready(t, kind):
        for d in range(1, chips):
            near_copy(4 * t + kind, chips - d).wait_recv()

    def load_rest():
        for i in range(QUARTERS):
            for copy in pre_copies(0, 0, i):
                copy.start()
        for i in range(QUARTERS):
            for copy in pre_copies(0, 1, i):
                copy.start()
            for copy in w_copies(1, i):
                copy.start()

    def load_next(t):
        for leg in range(2):
            for i in range(QUARTERS):
                for copy in pre_copies(t + 1, leg, i):
                    copy.start()

    def wait_w(leg, i):
        for copy in w_copies(leg, i):
            copy.wait()

    def wait_pre(t, leg, i):
        for copy in pre_copies(t, leg, i):
            copy.wait()

    def wait_small():
        for copy in small[3:]:
            copy.wait()

    def forward_step(t, kind, part, i):
        leg = ORDER[kind][1]
        cut = slice(i * quarter, (i + 1) * quarter)
        x = gather[4 * t + kind, part]
        hidden = jnp.maximum(jnp.dot(x, w_in[leg, :, cut], preferred_element_type=jnp.float32), 0.0)
        added = jnp.dot(hidden.astype(jnp.bfloat16), w_out[leg, cut, :], preferred_element_type=jnp.float32)
        if i == 0:
            acc[kind % 2, part] = added
        else:
            acc[kind % 2, part] += added

    def backward_step(t, kind, i):
        leg = ORDER[kind][1]
        cut = slice(i * quarter, (i + 1) * quarter)
        x = gather[4 * t + kind]
        up = lax.dot_general(
            x, w_out[leg, cut, :], (((1,), (1,)), ((), ())), preferred_element_type=jnp.float32
        )
        masked = jnp.where(pre[2 * t + leg, :, cut].astype(jnp.float32) > 0, up, 0.0).astype(jnp.bfloat16)
        added = lax.dot_general(
            masked, w_in[leg, :, cut], (((1,), (1,)), ((), ())), preferred_element_type=jnp.float32
        )
        if i == 0:
            acc[kind % 2] = added
        else:
            acc[kind % 2] += added

    small[0].wait()
    small[1].wait()
    enter(0, F0)
    small[2].wait()
    enter(0, B0)
    load_rest()

    def tick(t, carry):
        later(t, lambda: (finish(t - 1, B1), arrive(t, B0)))
        near_ready(t, F0)
        for i in range(QUARTERS):
            if i == 2:
                later(t, lambda: scatter_own(t - 1, F1))
            if i == 3:
                first(t, lambda: relay(0, F0))
            first(t, lambda: wait_w(0, i))
            forward_step(t, F0, near_rows, i)
        far_ready(t, F0)
        for i in range(QUARTERS):
            if i == 2:
                relay(t, B0)
                first(t, lambda: (wait_small(), enter(0, B1)))
                later(t, lambda: arrive(t, B1))
            forward_step(t, F0, far_rows, i)
        scatter_one(t, F0, 1)
        scatter_one(t, F0, 0)

        near_ready(t, B0)
        far_ready(t, B0)
        for i in range(QUARTERS):
            if i == 0:
                later(t, lambda: finish(t - 1, F1))
            if i == 1:
                scatter_two(t, F0)
            if i == 2:
                relay(t, B1)
            if i == 3:
                first(t, lambda: enter(0, F1))
                later(t, lambda: arrive(t, F1))
            wait_pre(t, 0, i)
            backward_step(t, B0, i)
        scatter_one(t, B0, 1)
        scatter_one(t, B0, 0)

        near_ready(t, B1)
        far_ready(t, B1)
        for i in range(QUARTERS):
            if i == 0:
                finish(t, F0)
            if i == 1:
                scatter_two(t, B0)
            if i == 2:
                relay(t, F1)
            if i == 3:
                more(t, lambda: arrive(t + 1, F0))
            first(t, lambda: wait_w(1, i))
            wait_pre(t, 1, i)
            backward_step(t, B1, i)
        scatter_one(t, B1, 1)
        scatter_one(t, B1, 0)

        near_ready(t, F1)
        far_ready(t, F1)
        for i in range(QUARTERS):
            if i == 0:
                more(t, lambda: load_next(t))
                finish(t, B0)
            if i == 2:
                scatter_two(t, B1)
            forward_step(t, F1, far_rows, i)
        scatter_one(t, F1, 1)
        for i in range(QUARTERS):
            if i == 0:
                more(t, lambda: relay(t + 1, F0))
            if i == 2:
                scatter_far(t, F1)
            forward_step(t, F1, near_rows, i)
        scatter_one(t, F1, 0)
        return carry

    lax.fori_loop(0, ticks, tick, 0)
    finish(ticks - 1, B1)
    scatter_own(ticks - 1, F1)
    finish(ticks - 1, F1)

    def drain(t, carry):
        for kind in range(4):
            p = 4 * t + kind
            for d in range(1, chips):
                far_copy(p, d).wait_send()
            for k in range(chips):
                near_copy(p, k).wait_send()
            s1_copy(p, 0).wait_send()
            s1_copy(p, 1).wait_send()
            for d in range(1, chips):
                s2_copy(p, d).wait_send()

            @pl.when(jnp.logical_and(t + 1 < ticks, hop_sends(kind)))
            def _():
                hop_copy(t, kind).wait_send()

            out_copy(t, kind).wait()
        return carry

    lax.fori_loop(0, ticks, drain, 0)


def flush(a_ref, g_ref, out_a_ref, out_g_ref, held, sem):
    pairs = ((a_ref, out_a_ref), (g_ref, out_g_ref))
    loads = [pltpu.make_async_copy(src, held.at[k], sem.at[0, k]) for k, (src, _) in enumerate(pairs)]
    stores = [pltpu.make_async_copy(held.at[k], dst, sem.at[1, k]) for k, (_, dst) in enumerate(pairs)]
    for copy in loads:
        copy.start()
    for load, store in zip(loads, stores):
        load.wait()
        store.start()
    for copy in stores:
        copy.wait()


def body(n, sections, w_in, w_out, gains, acts, grads, fresh_a, fresh_g, stash, pre):
    ticks = stash.shape[0]
    _, legs, d, ff = w_in.shape
    r = acts.shape[3]
    total_rows = n * r
    chips = n // 2
    passes = 4 * ticks
    bf16, f32 = jnp.bfloat16, jnp.float32
    any_spec = pl.BlockSpec(memory_space=pl.ANY)
    dma = pltpu.SemaphoreType.DMA
    far = max(chips - 1, 1)
    out = jax.ShapeDtypeStruct((ticks, legs, r, d), bf16)
    out_a, out_g = pl.pallas_call(
        functools.partial(kernel, n, sections, ticks),
        out_shape=(out, out),
        in_specs=[any_spec] * 9,
        out_specs=(any_spec, any_spec),
        scratch_shapes=[
            pltpu.VMEM((legs, d, ff), bf16),
            pltpu.VMEM((legs, ff, d), bf16),
            pltpu.VMEM((ticks * legs, total_rows, ff), bf16),
            pltpu.VMEM((legs, d), f32),
            pltpu.VMEM((2 * ticks, legs, r, d), bf16),
            pltpu.VMEM((2,) + (max(ticks - 1, 1), r, d), bf16),
            pltpu.VMEM((ticks, legs, r, d), bf16),
            pltpu.VMEM((passes, total_rows, d), bf16),
            pltpu.VMEM((2, total_rows, d), f32),
            pltpu.VMEM((passes, r, d), f32),
            pltpu.VMEM((passes, chips, r, d), bf16),
            pltpu.VMEM((passes, chips, r, d), bf16),
            pltpu.VMEM((passes, far, r, d), bf16),
            pltpu.VMEM((passes, far, r, d), bf16),
            pltpu.VMEM((passes, r, d), bf16),
            pltpu.VMEM((passes, r, d), bf16),
            dma((2, legs, QUARTERS)),
            dma((ticks * legs, QUARTERS, chips)),
            dma((6,)),
            dma((passes, far)),
            dma((passes, far)),
            dma((passes, chips)),
            dma((passes, chips)),
            dma((passes, 2)),
            dma((passes, 2)),
            dma((passes, far)),
            dma((passes, far)),
            dma((passes,)),
            dma((passes,)),
            dma((passes,)),
        ],
        compiler_params=pltpu.CompilerParams(
            collective_id=0, has_side_effects=True, vmem_limit_bytes=67043328
        ),
        name="relay",
    )(
        w_in[0], w_out[0], gains[0], acts[0, :, 0], grads[0, :, 0],
        fresh_a[:, 0], fresh_g[:, 0], stash[:, 0, :, 0], pre[:, 0, :, 0],
    )
    out_a, out_g = pl.pallas_call(
        flush,
        out_shape=(out, out),
        in_specs=[any_spec] * 2,
        out_specs=(any_spec, any_spec),
        scratch_shapes=[pltpu.VMEM((2,) + out.shape, bf16), dma((2, 2))],
        name="flush",
    )(out_a, out_g)
    return out_a[:, None, :, None], out_g[:, None, :, None]


def solution(mesh):
    return jax.shard_map(
        functools.partial(body, mesh.shape["mp"], mesh.shape["segment"]),
        mesh=mesh,
        in_specs=(
            P("segment", None, None, "mp"),
            P("segment", None, "mp", None),
            P("segment", None, None),
            P("segment", None, "tok", "mp", None),
            P("segment", None, "tok", "mp", None),
            P(None, "tok", "mp", None),
            P(None, "tok", "mp", None),
            P(None, "segment", None, "tok", "mp", None),
            P(None, "segment", None, "tok", None, "mp"),
        ),
        out_specs=(
            P(None, "segment", None, "tok", "mp", None),
            P(None, "segment", None, "tok", "mp", None),
        ),
        check_vma=False,
    )
```

time: 59.8 us -> 55.8 us (0.933)
  Pallas kernels: 59 us -> 55 us
    pallas_call x1, Pallas kernels: 57.2 us -> 53.3 us  [body(): pl.pallas_call(functools.partial(kernel, n, sections, ticks), out_shape=(...]
where the time goes in v1:
time: 55.8 us; the launch traced here: 55.7 us
  Pallas kernels  55 us (99%)
  between operations  0.64 us (1%)
    pallas_call x1, Pallas kernels, body(): pl.pallas_call(functools.partial(kernel, n, sections, ticks), out_shape=(...  53.3 us
    pallas_call x1, Pallas kernels, body(): pl.pallas_call(flush, out_shape=(out, out), in_specs=[any_spec] * 2, out_...  1.77 us

profile of v1, /device:TPU:0, one launch (start us, length us, event | category | flops | bytes accessed | tf_op | source)
XLA Modules:
  0.0 55.7 jit_solution(7480947476063072946)
XLA Ops:
  0.6 53.3 %relay.1 = (bf16[2,2,64,512]{3,2,1,0:T(8,128)(2,1)}, bf16[2,2,64,512]{3,2,1,0:T(8,128)(2,1)}) custom-call(bf16[2,512,8192]{2,1,0:T(8,128)(2,1)} %bitcast.15, bf16[2,8192,512]{2,1,0:T(8,128)(2,1)} %bitcast.16, f32[2,512]{1,0:T(2,128)} %bitcast.23, bf16[2,64,512]{2,1,0:T(8,128)(2,1)} %bitcast.19, bf16[2,64,512]{2,1,0:T(8,128)(2,1)} %bitcast.20, ...), custom_call_target="tpu_custom_call" | custom-call | tf_op jit(solution)/shard_map/relay/pallas_call | solution.py:444
  53.9 1.8 %flush.1 = (bf16[2,2,64,512]{3,2,1,0:T(8,128)(2,1)}, bf16[2,2,64,512]{3,2,1,0:T(8,128)(2,1)}) custom-call(bf16[2,2,64,512]{3,2,1,0:T(8,128)(2,1)} %get-tuple-element.6.a_ref, bf16[2,2,64,512]{3,2,1,0:T(8,128)(2,1)} %get-tuple-element.7.g_ref), custom_call_target="tpu_custom_call" | custom-call | tf_op jit(solution)/shard_map/flush/pallas_call | solution.py:489
